TPU v7x, 256 devices: a whole 4x4x8 slice. The times are simulated.
256 devices in a mesh: leaf: 32 (over z, x), rank: 4 (over y), rhs: 2 (over core).
Axes of the slice: x: 4, y: 4, z: 8, core: 2. Of those that a mesh axis runs over, the one named last changes fastest.
Arguments:
- rhs: float32 [65536, 512], P(('leaf', 'rank'), 'rhs'), parts along dimension 1, may hold values from -40 to 40
- order: int32 [65536], P(('leaf', 'rank')), may hold values from 0 to 65535, as said below
- diag: float32 [65536], P(('leaf', 'rank')), may hold values from 2 to 8
- blocks: bfloat16 [1536, 128, 128], P(('leaf', 'rank')), may hold values from -0.3125 to 0.3125
- near_rows: int32 [1536], P(('leaf', 'rank')), may hold values from 0 to 511, as said below
- near_cols: int32 [1536], P(('leaf', 'rank')), may hold values from 0 to 511, as said below
- gen_u: bfloat16 [5, 65536, 128], P(None, 'leaf', 'rank'), may hold values from -0.5 to 0.5
- gen_v: bfloat16 [5, 65536, 128], P(None, 'leaf', 'rank'), may hold values from -0.03125 to 0.03125
Outputs:
- solution: float32 [65536, 512], P(('leaf', 'rank'), 'rhs'), parts along dimension 1
- residual: float32 [65536, 512], P(('leaf', 'rank'), 'rhs'), parts along dimension 1
There are 2 independent parts, one for each index of `rhs`. A program takes and returns all parts, laid end to end along the dimension named above; an argument that names none is the same for every part. Nothing has to cross between parts.
Inputs may be any that keep to these rules, and one draw needn't show every extreme that they name: `order`: each aligned run of 512 entries is a permutation of the panel numbers of that run. `near_rows`: block k's row is one of the 4 block rows of the device that holds block k; every block row is named, at least once by a block whose column equals it. `near_cols`: block k's column lies in the same subtree of 2048 panels as its row, at most 4 block columns away from it.
All inputs are finite; a program needn't handle non-finite values.
Results may differ from a plain program's by a relative error of at most 0.0035.
Values may be sent and summed in bfloat16 or wider, within the bound.
A program may use at most 64 MiB of HBM per device.

v0:
```python
import jax
import jax.numpy as jnp
from jax import lax
from jax.sharding import PartitionSpec as P

EPSILON = 1e-06


def from_partner(value, axis, apart):
    mask = 2**apart
    pairs = [(source, source ^ mask) for source in range(lax.axis_size(axis))]
    return lax.ppermute(value, axis, pairs)


def local(rhs, order, diag, blocks, near_rows, near_cols, gen_u, gen_v):
    panel_count, columns_count = rhs.shape
    levels = gen_v.shape[0]
    leaf_panels = gen_v.shape[1]
    block_size = blocks.shape[1]
    rows_dev = panel_count // block_size
    rows_leaf = leaf_panels // block_size
    device = lax.axis_index(("leaf", "rank"))
    leaf_id = lax.axis_index("leaf")
    local_order = order - device * panel_count
    local_rows = near_rows - device * rows_dev
    local_cols = near_cols - leaf_id * rows_leaf
    selector = (jnp.arange(rows_dev, dtype=jnp.int32)[:, None] == local_rows[None, :]).astype(
        jnp.float32
    )

    def tree_sums(coeffs):
        partial_value = [coeffs[level] for level in range(levels)]
        sibling = []
        for level in range(levels):
            stacked = jnp.stack(partial_value[level:], 0)
            received = from_partner(stacked, "leaf", level)
            sibling.append(received[0])
            for upper in range(level + 1, levels):
                partial_value[upper] = partial_value[upper] + received[upper - level]
        return jnp.stack(sibling, 0)

    def apply(vector):
        narrow = vector.astype(jnp.bfloat16)
        subtree = lax.all_gather(narrow, "rank", axis=0, tiled=True)
        coeffs = jnp.einsum("lpk,pn->lkn", gen_v, subtree, preferred_element_type=jnp.float32)
        column_blocks = subtree.reshape(rows_leaf, block_size, columns_count)[local_cols]
        sibling = tree_sums(coeffs).astype(jnp.bfloat16)
        products = jnp.einsum(
            "kij,kjn->kin", blocks, column_blocks, preferred_element_type=jnp.float32
        )
        near = jnp.einsum(
            "rk,kin->rin", selector, products, precision=lax.Precision.HIGHEST
        ).reshape(panel_count, columns_count)
        far = lax.psum_scatter(
            jnp.einsum("lpk,lkn->pn", gen_u, sibling, preferred_element_type=jnp.float32),
            "rank",
            scatter_dimension=0,
            tiled=True,
        )
        return diag[:, None] * vector + near + far

    start = rhs[local_order]
    beta = jnp.sqrt(lax.psum(jnp.sum(start * start, axis=0), ("leaf", "rank")) + EPSILON)
    basis_one = start / beta
    image_one = apply(basis_one)
    h11 = lax.psum(jnp.sum(basis_one * image_one, axis=0), ("leaf", "rank"))
    rest_one = image_one - h11 * basis_one
    h21 = jnp.sqrt(lax.psum(jnp.sum(rest_one * rest_one, axis=0), ("leaf", "rank")) + EPSILON)
    basis_two = rest_one / h21
    image_two = apply(basis_two)
    h12, h22 = lax.psum(
        (jnp.sum(basis_one * image_two, axis=0), jnp.sum(basis_two * image_two, axis=0)),
        ("leaf", "rank"),
    )
    rest_two = image_two - h12 * basis_one - h22 * basis_two
    h32 = jnp.sqrt(lax.psum(jnp.sum(rest_two * rest_two, axis=0), ("leaf", "rank")) + EPSILON)
    r_one = jnp.sqrt(h11 * h11 + h21 * h21)
    cos_one = h11 / r_one
    sin_one = h21 / r_one
    top = cos_one * h12 + sin_one * h22
    low = cos_one * h22 - sin_one * h12
    r_two = jnp.sqrt(low * low + h32 * h32)
    y_two = low / r_two * (-sin_one * beta) / r_two
    y_one = (cos_one * beta - top * y_two) / r_one
    tree_solution = y_one * basis_one + y_two * basis_two
    tree_residual = (
        (beta - y_one * h11 - y_two * h12) * basis_one
        - (y_one * h21 + y_two * h22) * basis_two
        - y_two * rest_two
    )
    solution = jnp.zeros_like(rhs).at[local_order].set(tree_solution)
    residual = jnp.zeros_like(rhs).at[local_order].set(tree_residual)
    return (solution, residual)


def solution(mesh):
    in_specs = (
        P(("leaf", "rank"), "rhs"),
        P(("leaf", "rank")),
        P(("leaf", "rank")),
        P(("leaf", "rank"), None, None),
        P(("leaf", "rank")),
        P(("leaf", "rank")),
        P(None, "leaf", "rank"),
        P(None, "leaf", "rank"),
    )
    out_specs = (P(("leaf", "rank"), "rhs"), P(("leaf", "rank"), "rhs"))
    return jax.shard_map(local, mesh=mesh, in_specs=in_specs, out_specs=out_specs, check_vma=False)
```

profile of v0, /device:TPU:8, one launch (start us, length us, event | category | flops | bytes accessed | tf_op | source)
XLA Modules:
  0.0 1938.2 jit_solution(10514694611025003767)
XLA Ops:
  7.2 0.0 copy-start
  7.2 0.0 all-gather.3.cloned.1.call-start
  7.2 0.7 compare_select_fusion
  8.0 2.7 gather_fusion
  10.7 0.1 multiply_reduce_fusion.5
  10.8 346.4 %psum.42 = f32[256]{0:T(256)S(1)} all-reduce(f32[256]{0:T(256)S(1)} %multiply_reduce_fusion.5), channel_id=1, replica_groups=mesh['leaf'=32,'rank'=4,'rhs'=2] {'leaf','rank'}, use_global_device_ids=true, to_apply=%region_1.0 | all-reduce | flops 256 | bytes 2048 | tf_op jit(solution)/shard_map/psum | solution.py:63
  357.1 0.8 fusion.33
  357.9 0.0 all-gather.3.cloned.1.call-update
  357.9 0.0 reduce-scatter.3.cloned.1.call-start
  357.9 23.9 %all-gather.3.cloned.1.call-done = bf16[2048,256]{1,0:T(8,128)(2,1)} async-done(((bf16[512,256]{1,0:T(8,128)(2,1)}), bf16[2048,256]{1,0:T(8,128)(2,1)}) %all-gather.3.cloned.1.call-update) | async-done | bytes 1048592 | tf_op jit(solution)/shard_map/all_gather | solution.py:44
  381.9 1.6 fusion.37
  383.4 1.6 collective-permute-start
  385.0 3.9 collective-permute-done
  388.9 3.1 collective-permute-start.1
  391.9 3.5 collective-permute-done.1
  395.5 1.6 collective-permute-start.2
  397.1 3.8 collective-permute-done.2
  400.9 1.9 collective-permute-start.3
  402.8 3.3 collective-permute-done.3
  406.2 6.2 collective-permute-start.4
  412.4 1.7 collective-permute-done.4
  414.2 1.9 convolution_bitcast_fusion.1
  416.1 0.0 reduce-scatter.3.cloned.1.call-update
  416.1 0.0 all-gather.5.cloned.1.call-start
  416.2 0.6 gather_fusion.1
  416.8 0.2 copy-done.5
  417.1 1.6 fusion.35
  418.6 2.2 copy.17
  420.8 0.8 fusion.2
  421.7 0.1 copy.13
  421.8 27.5 %reduce-scatter.3.cloned.1.call-done = f32[512,256]{1,0:T(8,128)} async-done(((f32[2048,256]{1,0:T(8,128)}), f32[512,256]{1,0:T(8,128)}) %reduce-scatter.3.cloned.1.call-update) | async-done | bytes 524304 | tf_op jit(solution)/shard_map/reduce_scatter | solution.py:54
  449.3 1.2 multiply_reduce_fusion.4
  450.5 344.0 %psum.43 = f32[256]{0:T(256)S(1)} all-reduce(f32[256]{0:T(256)S(1)} %multiply_reduce_fusion.4), channel_id=1, replica_groups=mesh['leaf'=32,'rank'=4,'rhs'=2] {'leaf','rank'}, use_global_device_ids=true, to_apply=%region_4.0 | all-reduce | flops 256 | bytes 2048 | tf_op jit(solution)/shard_map/psum | solution.py:66
  794.5 1.2 multiply_reduce_fusion.3
  795.7 347.8 %psum.44 = f32[256]{0:T(256)S(1)} all-reduce(f32[256]{0:T(256)S(1)} %get-tuple-element.10), channel_id=1, replica_groups=mesh['leaf'=32,'rank'=4,'rhs'=2] {'leaf','rank'}, use_global_device_ids=true, to_apply=%region_6.0 | all-reduce | flops 256 | bytes 2048 | tf_op jit(solution)/shard_map/psum | solution.py:68
  1143.5 0.8 fusion.32
  1144.3 0.0 all-gather.5.cloned.1.call-update
  1144.3 0.0 reduce-scatter.5.cloned.1.call-start
  1144.4 20.1 %all-gather.5.cloned.1.call-done = bf16[2048,256]{1,0:T(8,128)(2,1)} async-done(((bf16[512,256]{1,0:T(8,128)(2,1)}), bf16[2048,256]{1,0:T(8,128)(2,1)}) %all-gather.5.cloned.1.call-update) | async-done | bytes 1048592 | tf_op jit(solution)/shard_map/all_gather | solution.py:44
  1164.5 1.6 fusion.38
  1166.0 1.6 collective-permute-start.5
  1167.6 3.9 collective-permute-done.5
  1171.5 3.1 collective-permute-start.6
  1174.6 3.5 collective-permute-done.6
  1178.1 1.6 collective-permute-start.7
  1179.7 3.8 collective-permute-done.7
  1183.5 1.9 collective-permute-start.8
  1185.4 3.3 collective-permute-done.8
  1188.8 6.4 collective-permute-start.9
  1195.2 1.7 collective-permute-done.9
  1196.9 1.9 convolution_bitcast_fusion
  1198.8 0.0 reduce-scatter.5.cloned.1.call-update
  1198.9 1.5 gather_fusion.2
  1200.4 1.6 fusion.36
  1202.1 1.9 copy.19
  1204.0 2.4 fusion
  1206.4 0.1 copy.15
  1206.5 25.5 %reduce-scatter.5.cloned.1.call-done = f32[512,256]{1,0:T(8,128)} async-done(((f32[2048,256]{1,0:T(8,128)}), f32[512,256]{1,0:T(8,128)}) %reduce-scatter.5.cloned.1.call-update) | async-done | bytes 524304 | tf_op jit(solution)/shard_map/reduce_scatter | solution.py:54
  1232.1 1.3 multiply_reduce_fusion.2
  1233.3 344.0 %all-reduce = (f32[256]{0:T(256)S(1)}, f32[256]{0:T(256)S(1)}) all-reduce(f32[256]{0:T(256)S(1)} %get-tuple-element.3, f32[256]{0:T(256)S(1)} %get-tuple-element.2), channel_id=1, replica_groups=mesh['leaf'=32,'rank'=4,'rhs'=2] {'leaf','rank'}, use_global_device_ids=true, to_apply=%region_11.0 | all-reduce | flops 512 | bytes 4096 | tf_op jit(solution)/shard_map/psum | solution.py:71
  1577.3 0.2 multiply_reduce_fusion
  1577.5 347.8 %psum.47 = f32[256]{0:T(256)S(1)} all-reduce(f32[256]{0:T(256)S(1)} %multiply_reduce_fusion), channel_id=1, replica_groups=mesh['leaf'=32,'rank'=4,'rhs'=2] {'leaf','rank'}, use_global_device_ids=true, to_apply=%region_13.0 | all-reduce | flops 256 | bytes 2048 | tf_op jit(solution)/shard_map/psum | solution.py:76
  1925.3 3.1 scatter_custom_fusion
  1928.4 3.2 scatter_custom_fusion.1
  (46 shorter events, 0.3 us)
Async XLA Ops:
  7.2 407.0 %copy-start = (bf16[5,2048,32]{1,2,0:T(8,128)(2,1)S(1)}, bf16[5,2048,32]{1,2,0:T(8,128)(2,1)}, u32[]{:S(2)}) copy-start(bf16[5,2048,32]{1,2,0:T(8,128)(2,1)} %param.14) | copy-start | bytes 1966084
  7.2 374.7 %all-gather.3.cloned.1.call-start = ((), (), s32[]{:S(2)}) async-start(), calls=%async_computation.2 | async-start | bytes 1310720 | tf_op jit(solution)/shard_map/all_gather | solution.py:44
  8.0 373.9 %copy-start.3 = (bf16[5,2048,32]{1,2,0:T(8,128)(2,1)S(1)}, bf16[5,2048,32]{1,2,0:T(8,128)(2,1)}, u32[]{:S(2)}) copy-start(bf16[5,2048,32]{1,2,0:T(8,128)(2,1)} %param.15) | copy-start | bytes 1966084
  357.9 91.4 %reduce-scatter.3.cloned.1.call-start = ((), (), s32[]{:S(2)}) async-start(), calls=%async_computation.3 | async-start | bytes 2621440 | tf_op jit(solution)/shard_map/reduce_scatter | solution.py:54
  383.4 5.4 collective-permute-start
  388.9 6.6 collective-permute-start.1
  395.5 5.4 collective-permute-start.2
  400.9 5.3 collective-permute-start.3
  406.2 8.0 collective-permute-start.4
  414.1 2.0 copy-start.7
  414.1 2.0 copy-start.8
  414.2 2.0 copy-start.1
  416.1 1.0 copy-start.5
  416.1 748.4 %all-gather.5.cloned.1.call-start = ((), (), s32[]{:S(2)}) async-start(), calls=%async_computation.4 | async-start | bytes 1310720 | tf_op jit(solution)/shard_map/all_gather | solution.py:44
  420.8 28.5 %copy-start.6 = (f32[512]{0:T(512)S(1)}, f32[512]{0:T(512)}, u32[]{:S(2)}) copy-start(f32[512]{0:T(512)} %param.10) | copy-start | bytes 6148
  421.8 742.7 %copy-start.4 = (bf16[5,2048,32]{1,2,0:T(8,128)(2,1)S(1)}, bf16[5,2048,32]{1,2,0:T(8,128)(2,1)}, u32[]{:S(2)}) copy-start(bf16[5,2048,32]{1,2,0:T(8,128)(2,1)} %param.15) | copy-start | bytes 1966084
  1144.3 87.8 %reduce-scatter.5.cloned.1.call-start = ((), (), s32[]{:S(2)}) async-start(), calls=%async_computation.5 | async-start | bytes 2621440 | tf_op jit(solution)/shard_map/reduce_scatter | solution.py:54
  1166.0 5.4 collective-permute-start.5
  1171.5 6.6 collective-permute-start.6
  1178.1 5.4 collective-permute-start.7
  1183.5 5.3 collective-permute-start.8
  1188.8 8.1 collective-permute-start.9
  1196.9 1.9 copy-start.2
Sparse Core Ops, SparseCore 0:
  358.0 23.7 all-gather.2
  416.2 33.0 reduce-scatter.2
  1144.4 20.0 all-gather.4
  1199.0 33.0 reduce-scatter.4
where the time goes:
time: 1940 us
  blocking collectives  1730 us (89%)
  waiting for transfers between devices  129 us (7%)
  starting transfers between devices  29.2 us (2%)
    psum x1, blocking collectives, local(): lax.psum(jnp.sum(rest_one * rest_one, axis=0), ('leaf', 'rank')) + EPSILON  348 us
    psum x1, blocking collectives, local(): lax.psum(jnp.sum(rest_two * rest_two, axis=0), ('leaf', 'rank')) + EPSILON  348 us
    psum x1, blocking collectives, local(): lax.psum(jnp.sum(start * start, axis=0), ('leaf', 'rank')) + EPSILON  346 us
    psum x1, blocking collectives, local(): lax.psum((jnp.sum(basis_one * image_two, axis=0), jnp.sum(basis_two * ima...  344 us
    psum x1, blocking collectives, local(): h11 = lax.psum(jnp.sum(basis_one * image_one, axis=0), ('leaf', 'rank'))  344 us
    reduce_scatter x2, waiting for transfers between devices, apply(): lax.psum_scatter(jnp.einsum('lpk,lkn->pn', gen_u, sibling, preferred_elem...  53 us
    all_gather x2, waiting for transfers between devices, apply(): subtree = lax.all_gather(narrow, 'rank', axis=0, tiled=True)  44 us
  transfers between devices with their start and end apart: 14, of which 14 were waited for; matrix products, arithmetic and copies ran while one was open for 1% of the time, Pallas kernels for 0%

commit v1 on v0

--- a/solution.py
+++ b/solution.py
@@ -69,8 +69,10 @@
     basis_two = rest_one / h21
     image_two = apply(basis_two)
     h12, h22 = lax.psum(
-        (jnp.sum(basis_one * image_two, axis=0), jnp.sum(basis_two * image_two, axis=0)),
-        ("leaf", "rank"),
+        lax.psum(
+            (jnp.sum(basis_one * image_two, axis=0), jnp.sum(basis_two * image_two, axis=0)), "leaf"
+        ),
+        "rank",
     )
     rest_two = image_two - h12 * basis_one - h22 * basis_two
     h32 = jnp.sqrt(lax.psum(jnp.sum(rest_two * rest_two, axis=0), ("leaf", "rank")) + EPSILON)

time: 1940 us -> 1670 us (0.86)
  blocking collectives: 1730 us -> 1470 us
    psum x1, blocking collectives: 344 us -> 75.1 us  [local(): lax.psum((jnp.sum(basis_one * image_two, axis=0), jnp.sum(basis_two * ima...]
where the time goes in v1:
time: 1670 us
  blocking collectives  1470 us (88%)
  waiting for transfers between devices  129 us (8%)
  starting transfers between devices  29.2 us (2%)
    psum x1, blocking collectives, local(): lax.psum(jnp.sum(rest_one * rest_one, axis=0), ('leaf', 'rank')) + EPSILON  348 us
    psum x1, blocking collectives, local(): lax.psum(jnp.sum(start * start, axis=0), ('leaf', 'rank')) + EPSILON  346 us
    psum x1, blocking collectives, local(): h11 = lax.psum(jnp.sum(basis_one * image_one, axis=0), ('leaf', 'rank'))  344 us
    psum x1, blocking collectives, local(): lax.psum(jnp.sum(rest_two * rest_two, axis=0), ('leaf', 'rank')) + EPSILON  343 us
    psum x1, blocking collectives, local(): lax.psum((jnp.sum(basis_one * image_two, axis=0), jnp.sum(basis_two * ima...  75.1 us
    reduce_scatter x2, waiting for transfers between devices, apply(): lax.psum_scatter(jnp.einsum('lpk,lkn->pn', gen_u, sibling, preferred_elem...  53 us
    all_gather x2, waiting for transfers between devices, apply(): subtree = lax.all_gather(narrow, 'rank', axis=0, tiled=True)  44 us
  transfers between devices with their start and end apart: 14, of which 14 were waited for; matrix products, arithmetic and copies ran while one was open for 1% of the time, Pallas kernels for 0%

profile of v1, /device:TPU:8, one launch (start us, length us, event | category | flops | bytes accessed | tf_op | source)
XLA Modules:
  0.0 1674.0 jit_solution(4806936930157717055)
XLA Ops:
  7.2 0.0 all-gather.3.cloned.1.call-start
  7.2 0.7 compare_select_fusion
  8.0 2.7 gather_fusion
  10.7 0.1 multiply_reduce_fusion.5
  10.8 346.4 %psum.56 = f32[256]{0:T(256)S(1)} all-reduce(f32[256]{0:T(256)S(1)} %multiply_reduce_fusion.5), channel_id=1, replica_groups=mesh['leaf'=32,'rank'=4,'rhs'=2] {'leaf','rank'}, use_global_device_ids=true, to_apply=%region_1.0 | all-reduce | flops 256 | bytes 2048 | tf_op jit(solution)/shard_map/psum | solution.py:63
  357.1 0.8 fusion.33
  357.9 0.0 all-gather.3.cloned.1.call-update
  357.9 0.0 reduce-scatter.3.cloned.1.call-start
  357.9 23.9 %all-gather.3.cloned.1.call-done = bf16[2048,256]{1,0:T(8,128)(2,1)} async-done(((bf16[512,256]{1,0:T(8,128)(2,1)}), bf16[2048,256]{1,0:T(8,128)(2,1)}) %all-gather.3.cloned.1.call-update) | async-done | bytes 1048592 | tf_op jit(solution)/shard_map/all_gather | solution.py:44
  381.9 1.6 fusion.37
  383.4 1.6 collective-permute-start
  385.0 3.9 collective-permute-done
  388.9 3.1 collective-permute-start.1
  391.9 3.5 collective-permute-done.1
  395.5 1.6 collective-permute-start.2
  397.1 3.8 collective-permute-done.2
  400.9 1.9 collective-permute-start.3
  402.8 3.3 collective-permute-done.3
  406.2 6.2 collective-permute-start.4
  412.4 1.7 collective-permute-done.4
  414.2 1.9 convolution_bitcast_fusion.1
  416.1 0.0 reduce-scatter.3.cloned.1.call-update
  416.1 0.0 all-gather.5.cloned.1.call-start
  416.2 0.6 gather_fusion.1
  416.8 0.2 copy-done.5
  417.1 1.6 fusion.35
  418.6 2.2 copy.17
  420.9 0.8 fusion.2
  421.7 0.1 copy.13
  421.8 27.5 %reduce-scatter.3.cloned.1.call-done = f32[512,256]{1,0:T(8,128)} async-done(((f32[2048,256]{1,0:T(8,128)}), f32[512,256]{1,0:T(8,128)}) %reduce-scatter.3.cloned.1.call-update) | async-done | bytes 524304 | tf_op jit(solution)/shard_map/reduce_scatter | solution.py:54
  449.3 1.2 multiply_reduce_fusion.4
  450.5 344.0 %psum.57 = f32[256]{0:T(256)S(1)} all-reduce(f32[256]{0:T(256)S(1)} %multiply_reduce_fusion.4), channel_id=1, replica_groups=mesh['leaf'=32,'rank'=4,'rhs'=2] {'leaf','rank'}, use_global_device_ids=true, to_apply=%region_4.0 | all-reduce | flops 256 | bytes 2048 | tf_op jit(solution)/shard_map/psum | solution.py:66
  794.5 1.2 multiply_reduce_fusion.3
  795.7 347.8 %psum.58 = f32[256]{0:T(256)S(1)} all-reduce(f32[256]{0:T(256)S(1)} %get-tuple-element.12), channel_id=1, replica_groups=mesh['leaf'=32,'rank'=4,'rhs'=2] {'leaf','rank'}, use_global_device_ids=true, to_apply=%region_6.0 | all-reduce | flops 256 | bytes 2048 | tf_op jit(solution)/shard_map/psum | solution.py:68
  1143.5 0.8 fusion.32
  1144.3 0.0 all-gather.5.cloned.1.call-update
  1144.3 0.0 reduce-scatter.5.cloned.1.call-start
  1144.4 20.1 %all-gather.5.cloned.1.call-done = bf16[2048,256]{1,0:T(8,128)(2,1)} async-done(((bf16[512,256]{1,0:T(8,128)(2,1)}), bf16[2048,256]{1,0:T(8,128)(2,1)}) %all-gather.5.cloned.1.call-update) | async-done | bytes 1048592 | tf_op jit(solution)/shard_map/all_gather | solution.py:44
  1164.5 1.6 fusion.38
  1166.0 1.6 collective-permute-start.5
  1167.6 3.8 collective-permute-done.5
  1171.5 3.1 collective-permute-start.6
  1174.6 3.5 collective-permute-done.6
  1178.1 1.6 collective-permute-start.7
  1179.7 3.8 collective-permute-done.7
  1183.5 1.9 collective-permute-start.8
  1185.5 3.3 collective-permute-done.8
  1188.8 6.4 collective-permute-start.9
  1195.2 1.7 collective-permute-done.9
  1196.9 1.9 convolution_bitcast_fusion
  1198.8 0.0 reduce-scatter.5.cloned.1.call-update
  1198.9 1.5 gather_fusion.2
  1200.4 1.6 fusion.36
  1202.1 1.9 copy.19
  1204.0 2.4 fusion
  1206.4 0.1 copy.15
  1206.5 25.6 %reduce-scatter.5.cloned.1.call-done = f32[512,256]{1,0:T(8,128)} async-done(((f32[2048,256]{1,0:T(8,128)}), f32[512,256]{1,0:T(8,128)}) %reduce-scatter.5.cloned.1.call-update) | async-done | bytes 524304 | tf_op jit(solution)/shard_map/reduce_scatter | solution.py:54
  1232.1 1.3 multiply_reduce_fusion.2
  1233.3 75.1 %all-reduce = (f32[256]{0:T(256)S(1)}, f32[256]{0:T(256)S(1)}) all-reduce(f32[256]{0:T(256)S(1)} %get-tuple-element.3, f32[256]{0:T(256)S(1)} %get-tuple-element.2), channel_id=1, replica_groups=mesh['leaf'=32,'rank'=4,'rhs'=2] {'leaf'}, use_global_device_ids=true, to_apply=%region_12.0 | all-reduce | flops 512 | bytes 4096 | tf_op jit(solution)/shard_map/psum | solution.py:72
  1308.4 9.5 all-reduce.1
  1317.9 0.2 multiply_reduce_fusion
  1318.1 343.0 %psum.63 = f32[256]{0:T(256)S(1)} all-reduce(f32[256]{0:T(256)S(1)} %multiply_reduce_fusion), channel_id=1, replica_groups=mesh['leaf'=32,'rank'=4,'rhs'=2] {'leaf','rank'}, use_global_device_ids=true, to_apply=%region_15.0 | all-reduce | flops 256 | bytes 2048 | tf_op jit(solution)/shard_map/psum | solution.py:78
  1661.1 3.1 scatter_custom_fusion
  1664.2 3.2 scatter_custom_fusion.1
  (47 shorter events, 0.3 us)
Async XLA Ops:
  7.2 407.0 %copy-start = (bf16[5,2048,32]{1,2,0:T(8,128)(2,1)S(1)}, bf16[5,2048,32]{1,2,0:T(8,128)(2,1)}, u32[]{:S(2)}) copy-start(bf16[5,2048,32]{1,2,0:T(8,128)(2,1)} %param.14) | copy-start | bytes 1966084
  7.2 374.7 %all-gather.3.cloned.1.call-start = ((), (), s32[]{:S(2)}) async-start(), calls=%async_computation.2 | async-start | bytes 1310720 | tf_op jit(solution)/shard_map/all_gather | solution.py:44
  8.0 373.9 %copy-start.3 = (bf16[5,2048,32]{1,2,0:T(8,128)(2,1)S(1)}, bf16[5,2048,32]{1,2,0:T(8,128)(2,1)}, u32[]{:S(2)}) copy-start(bf16[5,2048,32]{1,2,0:T(8,128)(2,1)} %param.15) | copy-start | bytes 1966084
  357.9 91.4 %reduce-scatter.3.cloned.1.call-start = ((), (), s32[]{:S(2)}) async-start(), calls=%async_computation.3 | async-start | bytes 2621440 | tf_op jit(solution)/shard_map/reduce_scatter | solution.py:54
  383.4 5.4 collective-permute-start
  388.9 6.6 collective-permute-start.1
  395.5 5.4 collective-permute-start.2
  400.9 5.3 collective-permute-start.3
  406.2 8.0 collective-permute-start.4
  414.1 2.0 copy-start.7
  414.1 2.0 copy-start.8
  414.2 2.1 copy-start.1
  416.1 1.0 copy-start.5
  416.1 748.4 %all-gather.5.cloned.1.call-start = ((), (), s32[]{:S(2)}) async-start(), calls=%async_computation.4 | async-start | bytes 1310720 | tf_op jit(solution)/shard_map/all_gather | solution.py:44
  420.8 28.4 %copy-start.6 = (f32[512]{0:T(512)S(1)}, f32[512]{0:T(512)}, u32[]{:S(2)}) copy-start(f32[512]{0:T(512)} %param.10) | copy-start | bytes 6148
  421.8 742.7 %copy-start.4 = (bf16[5,2048,32]{1,2,0:T(8,128)(2,1)S(1)}, bf16[5,2048,32]{1,2,0:T(8,128)(2,1)}, u32[]{:S(2)}) copy-start(bf16[5,2048,32]{1,2,0:T(8,128)(2,1)} %param.15) | copy-start | bytes 1966084
  1144.3 87.8 %reduce-scatter.5.cloned.1.call-start = ((), (), s32[]{:S(2)}) async-start(), calls=%async_computation.5 | async-start | bytes 2621440 | tf_op jit(solution)/shard_map/reduce_scatter | solution.py:54
  1166.0 5.4 collective-permute-start.5
  1171.5 6.6 collective-permute-start.6
  1178.1 5.4 collective-permute-start.7
  1183.5 5.3 collective-permute-start.8
  1188.8 8.1 collective-permute-start.9
  1196.9 1.9 copy-start.2
Sparse Core Ops, SparseCore 0:
  358.0 23.7 all-gather.2
  416.2 33.0 reduce-scatter.2
  1144.4 20.0 all-gather.4
  1199.0 33.0 reduce-scatter.4
